TPU v7x, 256 devices: a whole 4x4x8 slice. The times are simulated.
256 devices in a mesh: grp: 32 (over x, y, core), blk: 8 (over z).
Axes of the slice: x: 4, y: 4, z: 8, core: 2. Of those that a mesh axis runs over, the one named last changes fastest.
Arguments:
- tiles_near: bfloat16 [16384, 256, 256], P(('grp', 'blk')), may hold values from -0.078125 to 0.078125
- near_cols: int32 [256, 64], P(('grp', 'blk')), may hold values from 0 to 3
- tiles_far: bfloat16 [6144, 256, 256], P(('grp', 'blk')), may hold values from -0.078125 to 0.078125
- far_groups: int32 [256, 24], P(('grp', 'blk')), may hold values from 0 to 31, as said below
- need_blocks: int32 [256, 32], P(('grp', 'blk')), may hold values from -1 to 3, as said below
- start_vectors: bfloat16 [262144, 128], P(('grp', 'blk')), may hold values from -6 to 6
Outputs:
- vectors: float32 [262144, 128], P(('grp', 'blk'))
Inputs may be any that keep to these rules, and one draw needn't show every extreme that they name: need_blocks[d, h] is -1 for d's own group and for groups d reads nothing from, else a row block index below 4 of the device of group h at d's position along blk; every device reads from at least one other group. far_groups[d, t] is a group h with need_blocks[d, h] >= 0.
All inputs are finite; a program needn't handle non-finite values.
Results may differ from a plain program's by a relative error of at most 0.0029.
Values may be sent and summed in bfloat16 or wider, within the bound.
A program may use at most 128 MiB of HBM per device.

v0:
```python
import jax
import jax.numpy as jnp
from jax import lax
from jax.sharding import PartitionSpec as P

ITERS = 2


def per_device(tiles_near, near_cols, tiles_far, far_groups, need_blocks, start_vectors):
    tile_size = tiles_near.shape[1]
    vec_width = start_vectors.shape[1]
    blocks = start_vectors.shape[0] // tile_size
    group_size = lax.axis_size("blk")
    group_count = lax.axis_size("grp")
    per_source = tiles_near.shape[0] // (blocks * group_size)
    far_each = tiles_far.shape[0] // blocks
    near_tiles = tiles_near.reshape(blocks, group_size, per_source, tile_size, tile_size)
    near_index = near_cols.reshape(blocks, group_size, per_source)
    far_tiles = tiles_far.reshape(blocks, far_each, tile_size, tile_size)
    far_index = far_groups.reshape(blocks, far_each)
    wanted = need_blocks.reshape(group_count)
    total_rows = blocks * tile_size * group_size * group_count
    current = start_vectors
    vectors = start_vectors.astype(jnp.float32)
    for iteration in range(ITERS):
        local_rows = current.reshape(blocks, tile_size, vec_width)
        group_table = lax.all_gather(local_rows, "blk", axis=0, tiled=True)
        source_ids = jnp.arange(group_size, dtype=jnp.int32)[None, :, None]
        chosen = group_table[source_ids * blocks + near_index]
        near_part = jnp.einsum(
            "rmnij,rmnjk->rik", near_tiles, chosen, preferred_element_type=jnp.float32
        )
        everything = lax.all_gather(local_rows, "grp", axis=0, tiled=True)
        far_rows = everything[far_index * blocks + wanted[far_index]]
        far_part = jnp.einsum(
            "rnij,rnjk->rik", far_tiles, far_rows, preferred_element_type=jnp.float32
        )
        product = near_part + far_part
        flat_rows = product.reshape(blocks * tile_size, vec_width)
        local_gram = jnp.dot(
            flat_rows.T,
            flat_rows,
            precision=lax.Precision.HIGHEST,
            preferred_element_type=jnp.float32,
        )
        gram = lax.psum(local_gram, ("grp", "blk")) / total_rows
        factor = jnp.linalg.cholesky(gram)
        identity_matrix = jnp.eye(vec_width, dtype=jnp.float32)
        inverse = lax.linalg.triangular_solve(factor, identity_matrix, left_side=True, lower=True).T
        vectors = jnp.dot(
            flat_rows, inverse, precision=lax.Precision.HIGHEST, preferred_element_type=jnp.float32
        )
        current = vectors.astype(jnp.bfloat16)
    return vectors


def solution(mesh):
    in_specs = (
        P(("grp", "blk"), None, None),
        P(("grp", "blk"), None),
        P(("grp", "blk"), None, None),
        P(("grp", "blk"), None),
        P(("grp", "blk"), None),
        P(("grp", "blk"), None),
    )
    out_specs = P(("grp", "blk"), None)
    return jax.shard_map(
        per_device, mesh=mesh, in_specs=in_specs, out_specs=out_specs, check_vma=False
    )
```

profile of v0, /device:TPU:1, one launch (start us, length us, event | category | flops | bytes accessed | tf_op | source)
XLA Modules:
  0.0 777.3 jit_solution(7489281376360508679)
XLA Ops:
  10.1 1.4 gather_fusion.1
  11.6 1.3 reduce.11
  13.3 37.1 %all-gather.5.cloned.1.call-done = bf16[32,256,128]{2,1,0:T(8,128)(2,1)} async-done(((bf16[4,256,128]{2,1,0:T(8,128)(2,1)}), bf16[32,256,128]{2,1,0:T(8,128)(2,1)}) %all-gather.5.cloned.1.call-update) | async-done | bytes 2097168 | tf_op jit(solution)/shard_map/all_gather | solution.py:27
  50.4 4.6 gather_fusion
  55.0 58.5 %all-gather.7.cloned.1.call-done = bf16[128,256,128]{2,1,0:T(8,128)(2,1)} async-done(((bf16[4,256,128]{2,1,0:T(8,128)(2,1)}), bf16[128,256,128]{2,1,0:T(8,128)(2,1)}) %all-gather.7.cloned.1.call-update) | async-done | bytes 8388624 | tf_op jit(solution)/shard_map/all_gather | solution.py:33
  113.6 5.4 gather_fusion.2
  118.9 2.7 convolution_bitcast_fusion.1
  121.7 5.2 fusion.31
  129.0 2.0 copy.32
  131.0 235.3 %all-reduce.3.cloned.1.call-done = f32[128,128]{0,1:T(8,128)} async-done(((f32[128,128]{0,1:T(8,128)}), f32[128,128]{0,1:T(8,128)}) %all-reduce.3.cloned.1.call-update) | async-done | bytes 65552 | tf_op jit(solution)/shard_map/psum | solution.py:46
  368.1 11.7 %cholesky.44 = f32[128,128]{1,0:T(8,128)S(1)} custom-call(f32[128,128]{1,0:T(8,128)S(1)} %fusion.45), custom_call_target="Cholesky" | custom-call | tf_op jit(solution)/shard_map/jit(cholesky)/cholesky | solution.py:47
  381.2 9.8 %custom-call.6 = f32[1,128,128]{1,2,0:T(8,128)S(1)} custom-call(f32[1,128,128]{2,1,0:T(8,128)S(1)} %fusion.40), custom_call_target="InvertDiagBlocksLowerTriangular" | custom-call | tf_op jit(solution)/shard_map/triangular_solve/custom-call.0 | solution.py:49
  391.3 2.3 convolution_convert_fusion
  394.5 32.8 %all-gather.9.cloned.1.call-done = bf16[32,256,128]{2,1,0:T(8,128)(2,1)} async-done(((bf16[4,256,128]{2,1,0:T(8,128)(2,1)}), bf16[32,256,128]{2,1,0:T(8,128)(2,1)}) %all-gather.9.cloned.1.call-update) | async-done | bytes 2097168 | tf_op jit(solution)/shard_map/all_gather | solution.py:27
  427.3 4.6 gather_fusion.3
  432.0 58.4 %all-gather.11.cloned.1.call-done = bf16[128,256,128]{2,1,0:T(8,128)(2,1)} async-done(((bf16[4,256,128]{2,1,0:T(8,128)(2,1)}), bf16[128,256,128]{2,1,0:T(8,128)(2,1)}) %all-gather.11.cloned.1.call-update) | async-done | bytes 8388624 | tf_op jit(solution)/shard_map/all_gather | solution.py:33
  490.3 5.4 gather_fusion.4
  495.7 2.7 convolution_bitcast_fusion
  498.4 5.2 fusion.21
  505.7 2.0 copy.39
  507.7 235.3 %all-reduce.5.cloned.1.call-done = f32[128,128]{0,1:T(8,128)} async-done(((f32[128,128]{0,1:T(8,128)}), f32[128,128]{0,1:T(8,128)}) %all-reduce.5.cloned.1.call-update) | async-done | bytes 65552 | tf_op jit(solution)/shard_map/psum | solution.py:46
  744.9 11.7 %cholesky.55 = f32[128,128]{1,0:T(8,128)S(1)} custom-call(f32[128,128]{1,0:T(8,128)S(1)} %fusion.43), custom_call_target="Cholesky" | custom-call | tf_op jit(solution)/shard_map/jit(cholesky)/cholesky | solution.py:47
  757.9 9.8 %custom-call.7 = f32[1,128,128]{1,2,0:T(8,128)S(1)} custom-call(f32[1,128,128]{2,1,0:T(8,128)S(1)} %fusion.41), custom_call_target="InvertDiagBlocksLowerTriangular" | custom-call | tf_op jit(solution)/shard_map/triangular_solve/custom-call.0 | solution.py:49
  768.0 2.4 fusion.46
  (53 shorter events, 15.7 us)
Async XLA Ops:
  6.5 112.4 %copy-start = (bf16[24,256,256]{2,1,0:T(8,128)(2,1)S(1)}, bf16[24,256,256]{2,1,0:T(8,128)(2,1)}, u32[]{:S(2)}) copy-start(bf16[24,256,256]{2,1,0:T(8,128)(2,1)} %param.11) | copy-start | bytes 9437188
  6.5 43.8 %all-gather.5.cloned.1.call-start = ((), (), s32[]{:S(2)}) async-start(), calls=%async_computation | async-start | bytes 2359296 | tf_op jit(solution)/shard_map/all_gather | solution.py:27
  7.3 106.3 %all-gather.7.cloned.1.call-start = ((), (), s32[]{:S(2)}) async-start(), calls=%async_computation.1 | async-start | bytes 8650752 | tf_op jit(solution)/shard_map/all_gather | solution.py:33
  8.0 358.3 %all-reduce.3.cloned.1.call-start = ((), (), s32[]{:S(2)}) async-start(), calls=%async_computation.2 | async-start | bytes 131072 | tf_op jit(solution)/shard_map/psum | solution.py:46
  118.9 2.7 copy-start.4
  126.9 0.8 copy-start.1
  128.9 298.4 %all-gather.9.cloned.1.call-start = ((), (), s32[]{:S(2)}) async-start(), calls=%async_computation.3 | async-start | bytes 2359296 | tf_op jit(solution)/shard_map/all_gather | solution.py:27
  393.6 96.7 %all-gather.11.cloned.1.call-start = ((), (), s32[]{:S(2)}) async-start(), calls=%async_computation.4 | async-start | bytes 8650752 | tf_op jit(solution)/shard_map/all_gather | solution.py:33
  394.2 348.8 %all-reduce.5.cloned.1.call-start = ((), (), s32[]{:S(2)}) async-start(), calls=%async_computation.5 | async-start | bytes 131072 | tf_op jit(solution)/shard_map/psum | solution.py:46
  495.7 2.7 copy-start.3
  503.7 0.8 copy-start.2
Sparse Core Ops, SparseCore 0:
  9.1 41.1 all-gather.4
  52.9 60.5 all-gather.6
  129.1 237.2 all-reduce.2
  393.8 33.4 all-gather.8
  429.7 60.5 all-gather.10
  505.8 237.1 all-reduce.4
where the time goes:
time: 778 us; the launch traced here: 777 us
  waiting for transfers between devices  659 us (85%)
  other arithmetic  51.9 us (7%)
  local copies, waits for them, and re-layouts  28.3 us (4%)
  matrix products  23.6 us (3%)
  between operations  13.7 us (2%)
    psum x2, waiting for transfers between devices, per_device(): gram = lax.psum(local_gram, ('grp', 'blk')) / total_rows  471 us
    all_gather x2, waiting for transfers between devices, per_device(): everything = lax.all_gather(local_rows, 'grp', axis=0, tiled=True)  117 us
    all_gather x2, waiting for transfers between devices, per_device(): group_table = lax.all_gather(local_rows, 'blk', axis=0, tiled=True)  70 us
    another operation x6, other arithmetic, per_device(): factor = jnp.linalg.cholesky(gram)  24.8 us
    another operation x4, other arithmetic, per_device(): lax.linalg.triangular_solve(factor, identity_matrix, left_side=True, lowe...  20.9 us
  transfers between devices with their start and end apart: 6, of which 6 were waited for; matrix products, arithmetic and copies ran while one was open for 2% of the time, Pallas kernels for 0%

commit v1 on v0

--- a/solution.py
+++ b/solution.py
@@ -24,7 +24,18 @@
     vectors = start_vectors.astype(jnp.float32)
     for iteration in range(ITERS):
         local_rows = current.reshape(blocks, tile_size, vec_width)
-        group_table = lax.all_gather(local_rows, "blk", axis=0, tiled=True)
+        ways = lax.axis_size("blk")
+        up = [(d, (d + 1) % ways) for d in range(ways)]
+        down = [(d, (d - 1) % ways) for d in range(ways)]
+        earlier, later = ([local_rows], [local_rows])
+        for _ in range(ways // 2):
+            earlier.append(lax.ppermute(earlier[-1], "blk", up))
+        for _ in range((ways - 1) // 2):
+            later.append(lax.ppermute(later[-1], "blk", down))
+        line = jnp.concatenate([*earlier[::-1], *later[1:]], axis=0)
+        group_table = jnp.roll(
+            line, (lax.axis_index("blk") - ways // 2) * local_rows.shape[0], axis=0
+        )
         source_ids = jnp.arange(group_size, dtype=jnp.int32)[None, :, None]
         chosen = group_table[source_ids * blocks + near_index]
         near_part = jnp.einsum(

time: 778 us -> 694 us (0.89)
  waiting for transfers between devices: 659 us -> 543 us
  starting transfers between devices: 0.38 us -> 22.6 us
    all_gather x2, waiting for transfers between devices: 117 us -> 32.9 us  [per_device(): everything = lax.all_gather(local_rows, 'grp', axis=0, tiled=True)]
    all_gather x2 -> x0, waiting for transfers between devices: 70 us -> none  [per_device(): group_table = lax.all_gather(local_rows, 'blk', axis=0, tiled=True)]
    ppermute x0 -> x14, waiting for transfers between devices: none -> 38.9 us  [the longest x8 36.9 us: per_device(): earlier.append(lax.ppermute(earlier[-1], 'blk', up))]
    ppermute x0 -> x14, starting transfers between devices: none -> 22.3 us  [the longest x6 17.9 us: per_device(): later.append(lax.ppermute(later[-1], 'blk', down))]
  transfers between devices with their start and end apart: 6 -> 18, of which waited for: 6 -> 13; matrix products, arithmetic and copies ran while one was open for 2% -> 4% of each run, Pallas kernels for 0% -> 0%
where the time goes in v1:
time: 694 us; the launch traced here: 693 us
  waiting for transfers between devices  543 us (78%)
  other arithmetic  56 us (8%)
  local copies, waits for them, and re-layouts  34.7 us (5%)
  matrix products  23.6 us (3%)
  starting transfers between devices  22.6 us (3%)
  between operations  13.5 us (2%)
    psum x2, waiting for transfers between devices, per_device(): gram = lax.psum(local_gram, ('grp', 'blk')) / total_rows  470 us
    ppermute x8, waiting for transfers between devices, per_device(): earlier.append(lax.ppermute(earlier[-1], 'blk', up))  36.9 us
    all_gather x2, waiting for transfers between devices, per_device(): everything = lax.all_gather(local_rows, 'grp', axis=0, tiled=True)  32.9 us
    another operation x6, other arithmetic, per_device(): factor = jnp.linalg.cholesky(gram)  24.8 us
    another operation x4, other arithmetic, per_device(): lax.linalg.triangular_solve(factor, identity_matrix, left_side=True, lowe...  20.9 us
    ppermute x6, starting transfers between devices, per_device(): later.append(lax.ppermute(later[-1], 'blk', down))  17.9 us
  transfers between devices with their start and end apart: 18, of which 13 were waited for; matrix products, arithmetic and copies ran while one was open for 4% of the time, Pallas kernels for 0%

profile of v1, /device:TPU:1, one launch (start us, length us, event | category | flops | bytes accessed | tf_op | source)
XLA Modules:
  0.0 693.3 jit_solution(5461220925311783258)
XLA Ops:
  9.8 4.0 collective-permute-start.4
  15.8 4.2 collective-permute-done
  20.1 7.8 %collective-permute-done.1 = bf16[4,256,128]{2,1,0:T(8,128)(2,1)} collective-permute-done((bf16[4,256,128]{2,1,0:T(8,128)(2,1)S(1)}, bf16[4,256,128]{2,1,0:T(8,128)(2,1)}, u32[]{:S(2)}, u32[]{:S(2)}) %collective-permute-start.1) | collective-permute-done | bytes 262176 | tf_op jit(solution)/shard_map/ppermute | solution.py:32
  37.2 3.1 collective-permute-start.6
  50.0 4.7 gather_fusion
  54.7 17.4 %all-gather.3.cloned.1.call-done = bf16[128,256,128]{2,1,0:T(8,128)(2,1)} async-done(((bf16[4,256,128]{2,1,0:T(8,128)(2,1)}), bf16[128,256,128]{2,1,0:T(8,128)(2,1)}) %all-gather.3.cloned.1.call-update) | async-done | bytes 8388624 | tf_op jit(solution)/shard_map/all_gather | solution.py:44
  72.1 5.3 gather_fusion.2
  77.4 2.7 convolution_bitcast_fusion.1
  80.2 5.2 fusion.33
  89.7 235.1 %all-reduce.3.cloned.1.call-done = f32[128,128]{0,1:T(8,128)} async-done(((f32[128,128]{0,1:T(8,128)}), f32[128,128]{0,1:T(8,128)}) %all-reduce.3.cloned.1.call-update) | async-done | bytes 65552 | tf_op jit(solution)/shard_map/psum | solution.py:57
  326.6 11.7 %cholesky.44 = f32[128,128]{1,0:T(8,128)S(1)} custom-call(f32[128,128]{1,0:T(8,128)S(1)} %fusion.47), custom_call_target="Cholesky" | custom-call | tf_op jit(solution)/shard_map/jit(cholesky)/cholesky | solution.py:58
  339.6 9.8 %custom-call.6 = f32[1,128,128]{1,2,0:T(8,128)S(1)} custom-call(f32[1,128,128]{2,1,0:T(8,128)S(1)} %fusion.42), custom_call_target="InvertDiagBlocksLowerTriangular" | custom-call | tf_op jit(solution)/shard_map/triangular_solve/custom-call.0 | solution.py:60
  354.0 7.7 %collective-permute-done.7 = bf16[4,256,128]{2,1,0:T(8,128)(2,1)S(1)} collective-permute-done((bf16[4,256,128]{2,1,0:T(8,128)(2,1)}, bf16[4,256,128]{2,1,0:T(8,128)(2,1)S(1)}, u32[]{:S(2)}, u32[]{:S(2)}) %collective-permute-start.7) | collective-permute-done | bytes 262176 | tf_op jit(solution)/shard_map/ppermute | solution.py:32
  364.4 5.7 collective-permute-done.8
  372.8 4.8 collective-permute-done.9
  380.3 3.8 collective-permute-done.10
  386.5 4.6 gather_fusion.3
  391.1 15.6 %all-gather.5.cloned.1.call-done = bf16[128,256,128]{2,1,0:T(8,128)(2,1)} async-done(((bf16[4,256,128]{2,1,0:T(8,128)(2,1)}), bf16[128,256,128]{2,1,0:T(8,128)(2,1)}) %all-gather.5.cloned.1.call-update) | async-done | bytes 8388624 | tf_op jit(solution)/shard_map/all_gather | solution.py:44
  406.7 5.3 gather_fusion.4
  412.0 2.7 convolution_bitcast_fusion
  414.8 5.2 fusion.23
  424.1 235.3 %all-reduce.5.cloned.1.call-done = f32[128,128]{0,1:T(8,128)} async-done(((f32[128,128]{0,1:T(8,128)}), f32[128,128]{0,1:T(8,128)}) %all-reduce.5.cloned.1.call-update) | async-done | bytes 65552 | tf_op jit(solution)/shard_map/psum | solution.py:57
  661.2 11.7 %cholesky.55 = f32[128,128]{1,0:T(8,128)S(1)} custom-call(f32[128,128]{1,0:T(8,128)S(1)} %fusion.45), custom_call_target="Cholesky" | custom-call | tf_op jit(solution)/shard_map/jit(cholesky)/cholesky | solution.py:58
  674.3 9.8 %custom-call.7 = f32[1,128,128]{1,2,0:T(8,128)S(1)} custom-call(f32[1,128,128]{2,1,0:T(8,128)S(1)} %fusion.43), custom_call_target="InvertDiagBlocksLowerTriangular" | custom-call | tf_op jit(solution)/shard_map/triangular_solve/custom-call.0 | solution.py:60
  (99 shorter events, 56.4 us)
Async XLA Ops:
  6.5 70.9 %copy-start = (bf16[24,256,256]{2,1,0:T(8,128)(2,1)S(1)}, bf16[24,256,256]{2,1,0:T(8,128)(2,1)}, u32[]{:S(2)}) copy-start(bf16[24,256,256]{2,1,0:T(8,128)(2,1)} %param.13) | copy-start | bytes 9437188
  6.5 65.5 %all-gather.3.cloned.1.call-start = ((), (), s32[]{:S(2)}) async-start(), calls=%async_computation | async-start | bytes 8650752 | tf_op jit(solution)/shard_map/all_gather | solution.py:44
  7.3 317.5 %all-reduce.3.cloned.1.call-start = ((), (), s32[]{:S(2)}) async-start(), calls=%async_computation.1 | async-start | bytes 131072 | tf_op jit(solution)/shard_map/psum | solution.py:57
  7.3 12.7 %collective-permute-start = (bf16[4,256,128]{2,1,0:T(8,128)(2,1)}, bf16[4,256,128]{2,1,0:T(8,128)(2,1)S(1)}, u32[]{:S(2)}, u32[]{:S(2)}) collective-permute-start(bf16[4,256,128]{2,1,0:T(8,128)(2,1)} %bitcast.93), channel_id=1, source_target_pairs={{0,1},{1,2},{2,3},{3,4},{4,5},{5,6},{6,7},{7,0},{8,9},{9,10},{10,1... | collective-permute-start | bytes 786440 | tf_op jit(solution)/shard_map/ppermute | solution.py:32
  9.8 21.1 %collective-permute-start.4 = (bf16[4,256,128]{2,1,0:T(8,128)(2,1)}, bf16[4,256,128]{2,1,0:T(8,128)(2,1)}, u32[]{:S(2)}, u32[]{:S(2)}) collective-permute-start(bf16[4,256,128]{2,1,0:T(8,128)(2,1)} %bitcast.94), channel_id=1, source_target_pairs={{0,7},{1,0},{2,1},{3,2},{4,3},{5,4},{6,5},{7,6},{8,15},{9,8},{10,9... | collective-permute-start | bytes 786440 | tf_op jit(solution)/shard_map/ppermute | solution.py:34
  20.0 9.2 %copy-start.7 = (bf16[4,256,128]{2,1,0:T(8,128)(2,1)}, bf16[4,256,128]{2,1,0:T(8,128)(2,1)S(1)}, u32[]{:S(2)}) copy-start(bf16[4,256,128]{2,1,0:T(8,128)(2,1)S(1)} %collective-permute-done) | copy-start | bytes 786436
  20.0 7.9 %collective-permute-start.1 = (bf16[4,256,128]{2,1,0:T(8,128)(2,1)S(1)}, bf16[4,256,128]{2,1,0:T(8,128)(2,1)}, u32[]{:S(2)}, u32[]{:S(2)}) collective-permute-start(bf16[4,256,128]{2,1,0:T(8,128)(2,1)S(1)} %collective-permute-done), channel_id=1, source_target_pairs={{0,1},{1,2},{2,3},{3,4},{4,5},{5,6},{6,7},{7,0},{8,9},{9,10},{10,1... | collective-permute-start | bytes 786440 | tf_op jit(solution)/shard_map/ppermute | solution.py:32
  27.9 7.2 %collective-permute-start.2 = (bf16[4,256,128]{2,1,0:T(8,128)(2,1)}, bf16[4,256,128]{2,1,0:T(8,128)(2,1)}, u32[]{:S(2)}, u32[]{:S(2)}) collective-permute-start(bf16[4,256,128]{2,1,0:T(8,128)(2,1)} %collective-permute-done.1), channel_id=1, source_target_pairs={{0,1},{1,2},{2,3},{3,4},{4,5},{5,6},{6,7},{7,0},{8,9},{9,10},{10,1... | collective-permute-start | bytes 786440 | tf_op jit(solution)/shard_map/ppermute | solution.py:32
  29.2 16.6 %copy-start.6 = (bf16[1024,128]{1,0:T(8,128)(2,1)S(1)}, bf16[1024,128]{1,0:T(8,128)(2,1)}, u32[]{:S(2)}) copy-start(bf16[1024,128]{1,0:T(8,128)(2,1)} %param.16) | copy-start | bytes 786436
  30.9 6.3 collective-permute-start.5
  35.1 6.7 collective-permute-start.3
  37.2 10.6 %collective-permute-start.6 = (bf16[4,256,128]{2,1,0:T(8,128)(2,1)}, bf16[4,256,128]{2,1,0:T(8,128)(2,1)S(1)}, u32[]{:S(2)}, u32[]{:S(2)}) collective-permute-start(bf16[4,256,128]{2,1,0:T(8,128)(2,1)} %collective-permute-done.5), channel_id=1, source_target_pairs={{0,7},{1,0},{2,1},{3,2},{4,3},{5,4},{6,5},{7,6},{8,15},{9,8},{10,9... | collective-permute-start | bytes 786440 | tf_op jit(solution)/shard_map/ppermute | solution.py:34
  77.4 2.7 copy-start.4
  87.4 319.2 %all-gather.5.cloned.1.call-start = ((), (), s32[]{:S(2)}) async-start(), calls=%async_computation.2 | async-start | bytes 8650752 | tf_op jit(solution)/shard_map/all_gather | solution.py:44
  352.1 32.1 %copy-start.5 = (bf16[1024,128]{1,0:T(8,128)(2,1)S(1)}, bf16[1024,128]{1,0:T(8,128)(2,1)}, u32[]{:S(2)}) copy-start(bf16[1024,128]{1,0:T(8,128)(2,1)} %convolution_convert_fusion) | copy-start | bytes 786436
  352.1 307.3 %all-reduce.5.cloned.1.call-start = ((), (), s32[]{:S(2)}) async-start(), calls=%async_computation.3 | async-start | bytes 131072 | tf_op jit(solution)/shard_map/psum | solution.py:57
  352.1 9.6 %collective-permute-start.7 = (bf16[4,256,128]{2,1,0:T(8,128)(2,1)}, bf16[4,256,128]{2,1,0:T(8,128)(2,1)S(1)}, u32[]{:S(2)}, u32[]{:S(2)}) collective-permute-start(bf16[4,256,128]{2,1,0:T(8,128)(2,1)} %bitcast.87), channel_id=1, source_target_pairs={{0,1},{1,2},{2,3},{3,4},{4,5},{5,6},{6,7},{7,0},{8,9},{9,10},{10,1... | collective-permute-start | bytes 786440 | tf_op jit(solution)/shard_map/ppermute | solution.py:32
  361.7 8.4 %collective-permute-start.8 = (bf16[4,256,128]{2,1,0:T(8,128)(2,1)S(1)}, bf16[4,256,128]{2,1,0:T(8,128)(2,1)S(1)}, u32[]{:S(2)}, u32[]{:S(2)}) collective-permute-start(bf16[4,256,128]{2,1,0:T(8,128)(2,1)S(1)} %collective-permute-done.7), channel_id=1, source_target_pairs={{0,1},{1,2},{2,3},{3,4},{4,5},{5,6},{6,7},{7,0},{8,9},{9,10},{10,1... | collective-permute-start | bytes 786440 | tf_op jit(solution)/shard_map/ppermute | solution.py:32
  361.7 8.4 %collective-permute-start.11 = (bf16[4,256,128]{2,1,0:T(8,128)(2,1)}, bf16[4,256,128]{2,1,0:T(8,128)(2,1)S(1)}, u32[]{:S(2)}, u32[]{:S(2)}) collective-permute-start(bf16[4,256,128]{2,1,0:T(8,128)(2,1)} %bitcast.88), channel_id=1, source_target_pairs={{0,7},{1,0},{2,1},{3,2},{4,3},{5,4},{6,5},{7,6},{8,15},{9,8},{10,9... | collective-permute-start | bytes 786440 | tf_op jit(solution)/shard_map/ppermute | solution.py:34
  370.1 7.5 %collective-permute-start.9 = (bf16[4,256,128]{2,1,0:T(8,128)(2,1)S(1)}, bf16[4,256,128]{2,1,0:T(8,128)(2,1)S(1)}, u32[]{:S(2)}, u32[]{:S(2)}) collective-permute-start(bf16[4,256,128]{2,1,0:T(8,128)(2,1)S(1)} %collective-permute-done.8), channel_id=1, source_target_pairs={{0,1},{1,2},{2,3},{3,4},{4,5},{5,6},{6,7},{7,0},{8,9},{9,10},{10,1... | collective-permute-start | bytes 786440 | tf_op jit(solution)/shard_map/ppermute | solution.py:32
  370.1 7.5 %collective-permute-start.12 = (bf16[4,256,128]{2,1,0:T(8,128)(2,1)S(1)}, bf16[4,256,128]{2,1,0:T(8,128)(2,1)S(1)}, u32[]{:S(2)}, u32[]{:S(2)}) collective-permute-start(bf16[4,256,128]{2,1,0:T(8,128)(2,1)S(1)} %collective-permute-done.11), channel_id=1, source_target_pairs={{0,7},{1,0},{2,1},{3,2},{4,3},{5,4},{6,5},{7,6},{8,15},{9,8},{10,9... | collective-permute-start | bytes 786440 | tf_op jit(solution)/shard_map/ppermute | solution.py:34
  377.6 6.4 collective-permute-start.10
  377.6 6.7 collective-permute-start.13
  412.0 2.7 copy-start.3
  (2 other events, 1.6 us)
Sparse Core Ops, SparseCore 0:
  9.9 62.1 all-gather.2
  87.6 237.1 all-reduce.2
  352.2 54.4 all-gather.4
  422.2 237.2 all-reduce.4
